TPU v7x, 256 devices: a whole 4x4x8 slice. The times are simulated.
256 devices in a mesh: clip: 2 (over core), frame: 8 (over y, x_lo), band: 16 (over z, x_hi).
Axes of the slice: x: 4 (x_hi: 2, x_lo: 2; x = x_hi * 2 + x_lo), y: 4, z: 8, core: 2. Of those that a mesh axis runs over, the one named last changes fastest.
Arguments:
- latents: bfloat16 [4, 32, 64, 64, 320], P('clip', 'frame', 'band'), may hold values from -6 to 6
- spatial_kernel: bfloat16 [3, 3, 320, 320], replicated, may hold values from -0.109375 to 0.109375
- temporal_kernel: bfloat16 [3, 320, 320], replicated, may hold values from -0.1875 to 0.1875
- spatial_tangent: bfloat16 [3, 3, 320, 320], replicated, may hold values from -0.109375 to 0.109375
- temporal_tangent: bfloat16 [3, 320, 320], replicated, may hold values from -0.1875 to 0.1875
Outputs:
- curv_spatial: float32 [3, 3, 320, 320], replicated
- curv_temporal: float32 [3, 320, 320], replicated
All inputs are finite; a program needn't handle non-finite values.
Results may differ from a plain program's by a relative error of at most 0.00075.
Values may be sent and summed in bfloat16 or wider, within the bound.
No kernel may reach another device: no remote copies, remote signals or barrier semaphores. Data moves between devices by JAX's collectives and lax.ppermute only.
A program may use at most 128 MiB of HBM per device.

v0:
```python
import jax
import jax.numpy as jnp
from jax import lax
from jax.sharding import PartitionSpec as P


def padded_2(cells, sides, width):
    for axis, dim in sides:
        count = lax.axis_size(axis)
        ends = count - 1
        head = lax.slice_in_dim(cells, 0, width, axis=dim)
        tail = lax.slice_in_dim(cells, cells.shape[dim] - width, cells.shape[dim], axis=dim)
        cells = jnp.concatenate(
            [
                lax.ppermute(tail, axis, [(i, (i + 1) % count) for i in range(ends)]),
                cells,
                lax.ppermute(head, axis, [((i + 1) % count, i) for i in range(ends)]),
            ],
            axis=dim,
        )
    return cells


def forward_frames(framed, temporal_kernel, temporal_tangent):
    chans = framed.shape[-1]
    nframe = framed.shape[2] - 2
    act_pad = framed[0]
    dot_pad = framed[1]
    cat_act = jnp.concatenate([act_pad[:, k : k + nframe] for k in range(3)], axis=-1)
    cat_dot = jnp.concatenate([dot_pad[:, k : k + nframe] for k in range(3)], axis=-1)
    resid = jnp.einsum(
        "abrwk,kd->abrwd",
        cat_act,
        temporal_tangent.reshape(3 * chans, chans),
        preferred_element_type=jnp.float32,
    )
    resid = resid + jnp.einsum(
        "abrwk,kd->abrwd",
        cat_dot,
        temporal_kernel.reshape(3 * chans, chans),
        preferred_element_type=jnp.float32,
    )
    residual = resid.astype(jnp.bfloat16)
    grad_t = jnp.einsum("abrwk,abrwd->kd", cat_act, residual, preferred_element_type=jnp.float32)
    return (residual, grad_t)


def backward_frames(res_pad, temporal_kernel):
    nframe = res_pad.shape[1] - 2
    cat_res = jnp.concatenate([res_pad[:, 2 - k : 2 - k + nframe] for k in range(3)], axis=-1)
    back_w = jnp.concatenate([temporal_kernel[k].T for k in range(3)], axis=0)
    return jnp.einsum("abrwk,kd->abrwd", cat_res, back_w, preferred_element_type=jnp.float32)


def per_device(latents, spatial_kernel, temporal_kernel, spatial_tangent, temporal_tangent):
    chans = latents.shape[-1]
    rows = latents.shape[2]
    cols = latents.shape[3]
    padded = padded_2(latents, (("band", 2),), 1)
    padded = jnp.pad(padded, ((0, 0), (0, 0), (0, 0), (1, 1), (0, 0)))
    patches = jnp.concatenate(
        [padded[:, :, i : i + rows, j : j + cols, :] for i in range(3) for j in range(3)], axis=-1
    )
    both_w = jnp.concatenate(
        [spatial_kernel.reshape(9 * chans, chans), spatial_tangent.reshape(9 * chans, chans)],
        axis=1,
    )
    before = jnp.einsum("abrwk,kd->abrwd", patches, both_w, preferred_element_type=jnp.float32)
    hidden = before[..., :chans]
    tangent = before[..., chans:]
    sig = jax.nn.sigmoid(hidden)
    slope = sig * (1.0 + hidden * (1.0 - sig))
    active = (hidden * sig).astype(jnp.bfloat16)
    active_dot = (slope * tangent).astype(jnp.bfloat16)
    stacked = jnp.stack([active, active_dot])
    framed = padded_2(stacked, (("frame", 2),), 1)
    residual, grad_t = forward_frames(framed, temporal_kernel, temporal_tangent)
    res_pad = padded_2(residual, (("frame", 1),), 1)
    back = backward_frames(res_pad, temporal_kernel)
    hidden_bar = (slope * back).astype(jnp.bfloat16)
    grad_s = jnp.einsum("abrwk,abrwd->kd", patches, hidden_bar, preferred_element_type=jnp.float32)
    combined = jnp.concatenate(
        [grad_s.reshape(9, chans, chans), grad_t.reshape(3, chans, chans)], axis=0
    )
    total = lax.psum(combined, ("clip", "frame", "band"))
    devices = lax.axis_size("clip") * lax.axis_size("frame") * lax.axis_size("band")
    count = 1.0 * latents.shape[0] * latents.shape[1] * rows * cols * devices
    curv_spatial = (total[:9] * ((9.0 * chans) ** 0.5 / count)).reshape(3, 3, chans, chans)
    curv_temporal = total[9:] * ((3.0 * chans) ** 0.5 / count)
    return (curv_spatial, curv_temporal)


def solution(mesh):
    in_specs = (P("clip", "frame", "band", None, None), P(), P(), P(), P())
    out_specs = (P(), P())
    return jax.shard_map(
        per_device, mesh=mesh, in_specs=in_specs, out_specs=out_specs, check_vma=False
    )
```

profile of v0, /device:TPU:2, one launch (start us, length us, event | category | flops | bytes accessed | tf_op | source)
XLA Modules:
  0.0 461.5 jit_solution(8364531323663782129)
XLA Ops:
  7.2 0.0 copy-start
  7.2 0.0 all-reduce.3.cloned.1.call-start
  7.2 1.3 fusion.50
  8.5 4.1 collective-permute-start
  12.6 1.3 collective-permute-start.1
  13.9 15.5 %collective-permute-done = bf16[2,4,1,64,320]{4,3,2,1,0:T(8,128)(2,1)S(1)} collective-permute-done((bf16[2,4,1,64,320]{4,3,2,1,0:T(8,128)(2,1)S(1)}, bf16[2,4,1,64,320]{4,3,2,1,0:T(8,128)(2,1)S(1)}, u32[]{:S(2)}, u32[]{:S(2)}) %collective-permute-start) | collective-permute-done | bytes 327712 | tf_op jit(solution)/shard_map/ppermute | solution.py:15
  29.3 0.0 collective-permute-done.1
  29.3 2.4 fusion.23
  31.7 0.0 copy-start.2
  31.7 4.9 %fusion.46 = (bf16[2,4,4,64,320]{4,3,2,1,0:T(8,128)(2,1)}, bf16[2,4,4,64,320]{4,3,2,1,0:T(8,128)(2,1)}, bf16[2,4,4,64,320]{4,3,2,1,0:T(8,128)(2,1)}, bf16[2,4,4,...) fusion(bf16[2,4,6,66,320]{4,3,2,1,0:T(8,128)(2,1)S(1)} %fusion.23), kind=kLoop, calls=%fused_computation.61 | loop fusion | bytes 15728640 | tf_op jit(solution)/shard_map/slice | solution.py:62
  36.6 0.0 copy-done.2
  36.6 2.1 pad_maximum_fusion.5
  38.7 19.3 %concatenate.43 = bf16[2,4,4,64,2880]{4,3,2,1,0:T(8,128)(2,1)} concatenate(bf16[2,4,4,64,320]{4,3,2,1,0:T(8,128)(2,1)} %get-tuple-element.13, bf16[2,4,4,64,320]{4,3,2,1,0:T(8,128)(2,1)} %get-tuple-element.23, bf16[2,4,4,64,320]{4,3,2,1,0:T(8,128)(2,1)} %get-tuple-element.12, bf16[2,4,4,64,320]{4,3,2,1,0:T(8,128)(2,1)} %get-tuple-element.11, ...), dimensions={4} | concatenate | bytes 23592960 | tf_op jit(solution)/shard_map/concatenate | solution.py:61
  58.0 14.3 %fusion.15 = f32[2,4,4,64,640]{4,3,2,1,0:T(8,128)S(1)} fusion(bf16[2,4,4,64,2880]{4,3,2,1,0:T(8,128)(2,1)} %concatenate.43, bf16[2880,320]{1,0:T(8,128)(2,1)} %bitcast.56, bf16[2880,320]{1,0:T(8,128)(2,1)} %bitcast.57), kind=kOutput, calls=%fused_computation.22 | convolution fusion | flops 7557120000 | bytes 20725760 | tf_op jit(solution)/shard_map/abrwk,kd->abrwd/dot_general | solution.py:68
  72.3 0.0 copy-start.3
  72.3 1.5 fusion.30
  73.8 0.7 copy-done.3
  74.6 0.0 copy-start.4
  74.6 0.3 pad_maximum_fusion.10
  74.9 4.4 collective-permute-start.2
  79.2 2.1 collective-permute-start.3
  81.3 0.0 copy-done.4
  81.3 0.1 slice_bitcast_fusion.4
  81.4 15.7 %collective-permute-done.2 = bf16[2,2,1,4,64,320]{5,4,3,2,1,0:T(8,128)(2,1)S(1)} collective-permute-done((bf16[2,2,1,4,64,320]{5,4,3,2,1,0:T(8,128)(2,1)S(1)}, bf16[2,2,1,4,64,320]{5,4,3,2,1,0:T(8,128)(2,1)S(1)}, u32[]{:S(2)}, u32[]{:S(2)}) %collective-permute-start.2) | collective-permute-done | bytes 655392 | tf_op jit(solution)/shard_map/ppermute | solution.py:15
  97.1 15.9 %collective-permute-done.3 = bf16[2,2,1,4,64,320]{5,4,3,2,1,0:T(8,128)(2,1)S(1)} collective-permute-done((bf16[2,2,1,4,64,320]{5,4,3,2,1,0:T(8,128)(2,1)S(1)}, bf16[2,2,1,4,64,320]{5,4,3,2,1,0:T(8,128)(2,1)S(1)}, u32[]{:S(2)}, u32[]{:S(2)}) %collective-permute-start.3) | collective-permute-done | bytes 655392 | tf_op jit(solution)/shard_map/ppermute | solution.py:17
  113.0 1.3 pad_maximum_fusion.1
  114.3 0.8 slice_bitcast_fusion.1
  115.1 1.3 fusion.47
  116.4 2.4 fusion.8
  118.8 0.0 copy-done
  118.8 2.7 add_convert_fusion
  121.5 0.0 copy-start.5
  121.5 0.1 fusion.49
  121.6 3.3 collective-permute-start.4
  125.0 3.4 collective-permute-start.5
  128.4 2.8 fusion.31
  131.2 0.0 copy-done.5
  131.2 5.2 %collective-permute-done.4 = bf16[2,1,4,64,320]{4,3,2,1,0:T(8,128)(2,1)S(1)} collective-permute-done((bf16[2,1,4,64,320]{4,3,2,1,0:T(8,128)(2,1)S(1)}, bf16[2,1,4,64,320]{4,3,2,1,0:T(8,128)(2,1)S(1)}, u32[]{:S(2)}, u32[]{:S(2)}) %collective-permute-start.4) | collective-permute-done | bytes 327712 | tf_op jit(solution)/shard_map/ppermute | solution.py:17
  136.4 3.6 collective-permute-done.5
  140.1 0.0 copy-start.6
  140.1 0.7 copy-done.6
  140.8 17.6 %fusion.27 = f32[2880,320,1,1,1]{1,0,4,3,2:T(8,128)} fusion(bf16[2,4,4,64,2880]{4,3,2,1,0:T(8,128)(2,1)} %concatenate.43, bf16[2,4,4,64,320]{4,3,2,1,0:T(8,128)(2,1)} %copy-done.5, bf16[2,1,4,64,320]{4,3,2,1,0:T(8,128)(2,1)} %copy-done.6, bf16[2,1,4,64,320]{4,3,2,1,0:T(8,128)(2,1)S(1)} %collective-permute-done.4, ...), kind=kOutput, calls=%fused_computation.39 | convolution fusion | flops 5060567040 | bytes 21798912 | tf_op jit(solution)/shard_map/abrwk,abrwd->kd/dot_general | solution.py:81
  158.4 5.2 %pad_maximum_fusion = f32[12,320,320]{2,1,0:T(8,128)} fusion(f32[3,320,320]{2,1,0:T(8,128)S(1)} %bitcast.54, f32[9,320,320]{2,1,0:T(8,128)} %bitcast.52), kind=kLoop, calls=%fused_computation.2 | loop fusion | flops 1228800 | bytes 9830400 | tf_op jit(solution)/shard_map/concatenate | solution.py:82
  163.6 0.0 all-reduce.3.cloned.1.call-update
  163.6 283.7 %all-reduce.3.cloned.1.call-done = f32[12,320,320]{2,1,0:T(8,128)} async-done(((f32[12,320,320]{2,1,0:T(8,128)}), f32[12,320,320]{2,1,0:T(8,128)}) %all-reduce.3.cloned.1.call-update) | async-done | bytes 4915216 | tf_op jit(solution)/shard_map/psum | solution.py:85
  447.3 0.0 copy-start.1
  447.3 4.8 %slice_multiply_fusion = f32[9,320,320]{2,1,0:T(8,128)} fusion(f32[12,320,320]{2,1,0:T(8,128)} %all-reduce.3.cloned.1.call-done), kind=kLoop, calls=%fused_computation.5 | loop fusion | flops 921600 | bytes 7372800 | tf_op jit(solution)/shard_map/mul | solution.py:88
  452.1 2.6 slice_multiply_fusion.2
  454.7 0.0 copy-done.1
Async XLA Ops:
  7.2 111.7 %copy-start = (bf16[3,320,320]{2,1,0:T(8,128)(2,1)S(1)}, bf16[3,320,320]{2,1,0:T(8,128)(2,1)}, u32[]{:S(2)}) copy-start(bf16[3,320,320]{2,1,0:T(8,128)(2,1)} %param.9) | copy-start | bytes 1843204
  7.2 440.1 %all-reduce.3.cloned.1.call-start = ((), (), s32[]{:S(2)}) async-start(), calls=%async_computation | async-start | bytes 11796480 | tf_op jit(solution)/shard_map/psum | solution.py:85
  8.5 20.8 %collective-permute-start = (bf16[2,4,1,64,320]{4,3,2,1,0:T(8,128)(2,1)S(1)}, bf16[2,4,1,64,320]{4,3,2,1,0:T(8,128)(2,1)S(1)}, u32[]{:S(2)}, u32[]{:S(2)}) collective-permute-start(bf16[2,4,1,64,320]{4,3,2,1,0:T(8,128)(2,1)S(1)} %get-tuple-element.24), channel_id=1, source_target_pairs={{0,1},{1,2},{2,3},{3,4},{4,5},{5,6},{6,7},{7,8},{8,9},{9,10},{10,1... | collective-permute-start | bytes 983048 | tf_op jit(solution)/shard_map/ppermute | solution.py:15
  12.6 16.8 %collective-permute-start.1 = (bf16[2,4,1,64,320]{4,3,2,1,0:T(8,128)(2,1)S(1)}, bf16[2,4,1,64,320]{4,3,2,1,0:T(8,128)(2,1)S(1)}, u32[]{:S(2)}, u32[]{:S(2)}) collective-permute-start(bf16[2,4,1,64,320]{4,3,2,1,0:T(8,128)(2,1)S(1)} %get-tuple-element.25), channel_id=1, source_target_pairs={{1,0},{2,1},{3,2},{4,3},{5,4},{6,5},{7,6},{8,7},{9,8},{10,9},{11,1... | collective-permute-start | bytes 983048 | tf_op jit(solution)/shard_map/ppermute | solution.py:17
  31.7 4.9 %copy-start.2 = (bf16[2,4,4,64,320]{4,3,2,1,0:T(8,128)(2,1)S(1)}, bf16[2,4,4,64,320]{4,3,2,1,0:T(8,128)(2,1)}, u32[]{:S(2)}) copy-start(bf16[2,4,4,64,320]{4,3,2,1,0:T(8,128)(2,1)} %param.5) | copy-start | bytes 3932164
  72.3 2.3 copy-start.3
  74.6 6.8 %copy-start.4 = (bf16[3,320,320]{2,1,0:T(8,128)(2,1)S(1)}, bf16[3,320,320]{2,1,0:T(8,128)(2,1)}, u32[]{:S(2)}) copy-start(bf16[3,320,320]{2,1,0:T(8,128)(2,1)} %param.7) | copy-start | bytes 1843204
  74.9 22.3 %collective-permute-start.2 = (bf16[2,2,1,4,64,320]{5,4,3,2,1,0:T(8,128)(2,1)S(1)}, bf16[2,2,1,4,64,320]{5,4,3,2,1,0:T(8,128)(2,1)S(1)}, u32[]{:S(2)}, u32[]{:S(2)}) collective-permute-start(bf16[2,2,1,4,64,320]{5,4,3,2,1,0:T(8,128)(2,1)S(1)} %get-tuple-element.6), channel_id=1, source_target_pairs={{0,16},{16,32},{32,48},{48,64},{64,80},{80,96},{96,112},{1,17},{17... | collective-permute-start | bytes 1966088 | tf_op jit(solution)/shard_map/ppermute | solution.py:15
  79.2 33.8 %collective-permute-start.3 = (bf16[2,2,1,4,64,320]{5,4,3,2,1,0:T(8,128)(2,1)S(1)}, bf16[2,2,1,4,64,320]{5,4,3,2,1,0:T(8,128)(2,1)S(1)}, u32[]{:S(2)}, u32[]{:S(2)}) collective-permute-start(bf16[2,2,1,4,64,320]{5,4,3,2,1,0:T(8,128)(2,1)S(1)} %get-tuple-element.7), channel_id=1, source_target_pairs={{16,0},{32,16},{48,32},{64,48},{80,64},{96,80},{112,96},{17,1},{33... | collective-permute-start | bytes 1966088 | tf_op jit(solution)/shard_map/ppermute | solution.py:17
  121.5 9.7 %copy-start.5 = (bf16[2,4,4,64,320]{4,3,2,1,0:T(8,128)(2,1)}, bf16[2,4,4,64,320]{4,3,2,1,0:T(8,128)(2,1)S(1)}, u32[]{:S(2)}) copy-start(bf16[2,4,4,64,320]{4,3,2,1,0:T(8,128)(2,1)S(1)} %add_convert_fusion) | copy-start | bytes 3932164
  121.6 14.8 %collective-permute-start.4 = (bf16[2,1,4,64,320]{4,3,2,1,0:T(8,128)(2,1)S(1)}, bf16[2,1,4,64,320]{4,3,2,1,0:T(8,128)(2,1)S(1)}, u32[]{:S(2)}, u32[]{:S(2)}) collective-permute-start(bf16[2,1,4,64,320]{4,3,2,1,0:T(8,128)(2,1)S(1)} %get-tuple-element.20), channel_id=1, source_target_pairs={{16,0},{32,16},{48,32},{64,48},{80,64},{96,80},{112,96},{17,1},{33... | collective-permute-start | bytes 983048 | tf_op jit(solution)/shard_map/ppermute | solution.py:17
  125.0 15.1 %collective-permute-start.5 = (bf16[2,1,4,64,320]{4,3,2,1,0:T(8,128)(2,1)S(1)}, bf16[2,1,4,64,320]{4,3,2,1,0:T(8,128)(2,1)S(1)}, u32[]{:S(2)}, u32[]{:S(2)}) collective-permute-start(bf16[2,1,4,64,320]{4,3,2,1,0:T(8,128)(2,1)S(1)} %get-tuple-element.21), channel_id=1, source_target_pairs={{0,16},{16,32},{32,48},{48,64},{64,80},{80,96},{96,112},{1,17},{17... | collective-permute-start | bytes 983048 | tf_op jit(solution)/shard_map/ppermute | solution.py:15
  140.1 0.7 copy-start.6
  447.3 7.4 %copy-start.1 = (bf16[3,320,320]{2,1,0:T(8,128)(2,1)S(1)}, bf16[3,320,320]{2,1,0:T(8,128)(2,1)}, u32[]{:S(2)}) copy-start(bf16[3,320,320]{2,1,0:T(8,128)(2,1)} %param.9) | copy-start | bytes 1843204
Sparse Core Ops, SparseCore 0:
  163.8 283.4 all-reduce.2
where the time goes:
time: 463 us; the launch traced here: 462 us
  waiting for transfers between devices  340 us (73%)
  matrix products  39.7 us (9%)
  local copies, waits for them, and re-layouts  29.2 us (6%)
  other arithmetic  20.2 us (4%)
  starting transfers between devices  18.6 us (4%)
  between operations  14.2 us (3%)
    psum x1, waiting for transfers between devices, per_device(): total = lax.psum(combined, ('clip', 'frame', 'band'))  284 us
    ppermute x3, waiting for transfers between devices, padded_2(): lax.ppermute(tail, axis, [(i, (i + 1) % count) for i in range(ends)])  34.8 us
    ppermute x3, waiting for transfers between devices, padded_2(): lax.ppermute(head, axis, [((i + 1) % count, i) for i in range(ends)])  21.1 us
    concatenate x1, local copies, waits for them, and re-layouts, per_device(): jnp.concatenate([padded[:, :, i:i + rows, j:j + cols, :] for i in range(3...  19.3 us
    dot_general x1, matrix products, per_device(): jnp.einsum('abrwk,abrwd->kd', patches, hidden_bar, preferred_element_type...  17.6 us
    dot_general x1, matrix products, per_device(): jnp.einsum('abrwk,kd->abrwd', patches, both_w, preferred_element_type=jnp...  14.3 us
    ppermute x3, starting transfers between devices, padded_2(): lax.ppermute(tail, axis, [(i, (i + 1) % count) for i in range(ends)])  11.8 us
  transfers between devices with their start and end apart: 7, of which 6 were waited for; matrix products, arithmetic and copies ran while one was open for 1% of the time, Pallas kernels for 0%

commit v1 on v0

--- a/solution.py
+++ b/solution.py
@@ -82,7 +82,7 @@
     combined = jnp.concatenate(
         [grad_s.reshape(9, chans, chans), grad_t.reshape(3, chans, chans)], axis=0
     )
-    total = lax.psum(combined, ("clip", "frame", "band"))
+    total = lax.psum(lax.psum(combined, ("frame", "band")), "clip")
     devices = lax.axis_size("clip") * lax.axis_size("frame") * lax.axis_size("band")
     count = 1.0 * latents.shape[0] * latents.shape[1] * rows * cols * devices
     curv_spatial = (total[:9] * ((9.0 * chans) ** 0.5 / count)).reshape(3, 3, chans, chans)

time: 463 us -> 473 us (1.022)
  waiting for transfers between devices: 340 us -> 348 us
    psum x1 -> x2, waiting for transfers between devices: 284 us -> 292 us  [per_device(): total = lax.psum(lax.psum(combined, ('frame', 'band')), 'clip')]
  transfers between devices with their start and end apart: 7 -> 8, of which waited for: 6 -> 7; matrix products, arithmetic and copies ran while one was open for 1% -> 1% of each run, Pallas kernels for 0% -> 0%
where the time goes in v1:
time: 473 us; the launch traced here: 470 us
  waiting for transfers between devices  348 us (74%)
  matrix products  39.7 us (8%)
  local copies, waits for them, and re-layouts  29.2 us (6%)
  other arithmetic  20.2 us (4%)
  starting transfers between devices  18.6 us (4%)
  between operations  14.2 us (3%)
    psum x2, waiting for transfers between devices, per_device(): total = lax.psum(lax.psum(combined, ('frame', 'band')), 'clip')  292 us
    ppermute x3, waiting for transfers between devices, padded_2(): lax.ppermute(tail, axis, [(i, (i + 1) % count) for i in range(ends)])  34.8 us
    ppermute x3, waiting for transfers between devices, padded_2(): lax.ppermute(head, axis, [((i + 1) % count, i) for i in range(ends)])  21.1 us
    concatenate x1, local copies, waits for them, and re-layouts, per_device(): jnp.concatenate([padded[:, :, i:i + rows, j:j + cols, :] for i in range(3...  19.3 us
    dot_general x1, matrix products, per_device(): jnp.einsum('abrwk,abrwd->kd', patches, hidden_bar, preferred_element_type...  17.6 us
    dot_general x1, matrix products, per_device(): jnp.einsum('abrwk,kd->abrwd', patches, both_w, preferred_element_type=jnp...  14.3 us
    ppermute x3, starting transfers between devices, padded_2(): lax.ppermute(tail, axis, [(i, (i + 1) % count) for i in range(ends)])  11.8 us
  transfers between devices with their start and end apart: 8, of which 7 were waited for; matrix products, arithmetic and copies ran while one was open for 1% of the time, Pallas kernels for 0%

profile of v1, /device:TPU:2, one launch (start us, length us, event | category | flops | bytes accessed | tf_op | source)
XLA Modules:
  0.0 470.1 jit_solution(7393552117274042919)
XLA Ops:
  7.2 0.0 copy-start
  7.2 0.0 all-reduce.4.cloned.1.call-start
  7.2 1.3 fusion.50
  8.5 4.1 collective-permute-start
  12.6 1.3 collective-permute-start.1
  13.9 15.5 %collective-permute-done = bf16[2,4,1,64,320]{4,3,2,1,0:T(8,128)(2,1)S(1)} collective-permute-done((bf16[2,4,1,64,320]{4,3,2,1,0:T(8,128)(2,1)S(1)}, bf16[2,4,1,64,320]{4,3,2,1,0:T(8,128)(2,1)S(1)}, u32[]{:S(2)}, u32[]{:S(2)}) %collective-permute-start) | collective-permute-done | bytes 327712 | tf_op jit(solution)/shard_map/ppermute | solution.py:15
  29.3 0.0 collective-permute-done.1
  29.3 2.4 fusion.23
  31.7 0.0 copy-start.2
  31.7 4.9 %fusion.46 = (bf16[2,4,4,64,320]{4,3,2,1,0:T(8,128)(2,1)}, bf16[2,4,4,64,320]{4,3,2,1,0:T(8,128)(2,1)}, bf16[2,4,4,64,320]{4,3,2,1,0:T(8,128)(2,1)}, bf16[2,4,4,...) fusion(bf16[2,4,6,66,320]{4,3,2,1,0:T(8,128)(2,1)S(1)} %fusion.23), kind=kLoop, calls=%fused_computation.61 | loop fusion | bytes 15728640 | tf_op jit(solution)/shard_map/slice | solution.py:62
  36.6 0.0 copy-done.2
  36.6 2.1 pad_maximum_fusion.5
  38.7 19.3 %concatenate.43 = bf16[2,4,4,64,2880]{4,3,2,1,0:T(8,128)(2,1)} concatenate(bf16[2,4,4,64,320]{4,3,2,1,0:T(8,128)(2,1)} %get-tuple-element.13, bf16[2,4,4,64,320]{4,3,2,1,0:T(8,128)(2,1)} %get-tuple-element.23, bf16[2,4,4,64,320]{4,3,2,1,0:T(8,128)(2,1)} %get-tuple-element.12, bf16[2,4,4,64,320]{4,3,2,1,0:T(8,128)(2,1)} %get-tuple-element.11, ...), dimensions={4} | concatenate | bytes 23592960 | tf_op jit(solution)/shard_map/concatenate | solution.py:61
  58.0 14.3 %fusion.15 = f32[2,4,4,64,640]{4,3,2,1,0:T(8,128)S(1)} fusion(bf16[2,4,4,64,2880]{4,3,2,1,0:T(8,128)(2,1)} %concatenate.43, bf16[2880,320]{1,0:T(8,128)(2,1)} %bitcast.56, bf16[2880,320]{1,0:T(8,128)(2,1)} %bitcast.57), kind=kOutput, calls=%fused_computation.22 | convolution fusion | flops 7557120000 | bytes 20725760 | tf_op jit(solution)/shard_map/abrwk,kd->abrwd/dot_general | solution.py:68
  72.3 0.0 copy-start.3
  72.3 1.5 fusion.30
  73.8 0.7 copy-done.3
  74.6 0.0 copy-start.4
  74.6 0.3 pad_maximum_fusion.10
  74.9 4.4 collective-permute-start.2
  79.2 2.1 collective-permute-start.3
  81.3 0.0 copy-done.4
  81.3 0.1 slice_bitcast_fusion.4
  81.4 15.7 %collective-permute-done.2 = bf16[2,2,1,4,64,320]{5,4,3,2,1,0:T(8,128)(2,1)S(1)} collective-permute-done((bf16[2,2,1,4,64,320]{5,4,3,2,1,0:T(8,128)(2,1)S(1)}, bf16[2,2,1,4,64,320]{5,4,3,2,1,0:T(8,128)(2,1)S(1)}, u32[]{:S(2)}, u32[]{:S(2)}) %collective-permute-start.2) | collective-permute-done | bytes 655392 | tf_op jit(solution)/shard_map/ppermute | solution.py:15
  97.1 15.9 %collective-permute-done.3 = bf16[2,2,1,4,64,320]{5,4,3,2,1,0:T(8,128)(2,1)S(1)} collective-permute-done((bf16[2,2,1,4,64,320]{5,4,3,2,1,0:T(8,128)(2,1)S(1)}, bf16[2,2,1,4,64,320]{5,4,3,2,1,0:T(8,128)(2,1)S(1)}, u32[]{:S(2)}, u32[]{:S(2)}) %collective-permute-start.3) | collective-permute-done | bytes 655392 | tf_op jit(solution)/shard_map/ppermute | solution.py:17
  113.0 1.3 pad_maximum_fusion.1
  114.3 0.8 slice_bitcast_fusion.1
  115.1 1.3 fusion.47
  116.4 2.4 fusion.8
  118.8 0.0 copy-done
  118.8 2.7 add_convert_fusion
  121.5 0.0 copy-start.5
  121.5 0.1 fusion.49
  121.6 3.3 collective-permute-start.4
  125.0 3.4 collective-permute-start.5
  128.4 2.8 fusion.31
  131.2 0.0 copy-done.5
  131.2 5.2 %collective-permute-done.4 = bf16[2,1,4,64,320]{4,3,2,1,0:T(8,128)(2,1)S(1)} collective-permute-done((bf16[2,1,4,64,320]{4,3,2,1,0:T(8,128)(2,1)S(1)}, bf16[2,1,4,64,320]{4,3,2,1,0:T(8,128)(2,1)S(1)}, u32[]{:S(2)}, u32[]{:S(2)}) %collective-permute-start.4) | collective-permute-done | bytes 327712 | tf_op jit(solution)/shard_map/ppermute | solution.py:17
  136.4 3.6 collective-permute-done.5
  140.1 0.0 copy-start.6
  140.1 0.7 copy-done.6
  140.8 17.6 %fusion.27 = f32[2880,320,1,1,1]{1,0,4,3,2:T(8,128)} fusion(bf16[2,4,4,64,2880]{4,3,2,1,0:T(8,128)(2,1)} %concatenate.43, bf16[2,4,4,64,320]{4,3,2,1,0:T(8,128)(2,1)} %copy-done.5, bf16[2,1,4,64,320]{4,3,2,1,0:T(8,128)(2,1)} %copy-done.6, bf16[2,1,4,64,320]{4,3,2,1,0:T(8,128)(2,1)S(1)} %collective-permute-done.4, ...), kind=kOutput, calls=%fused_computation.39 | convolution fusion | flops 5060567040 | bytes 21798912 | tf_op jit(solution)/shard_map/abrwk,abrwd->kd/dot_general | solution.py:81
  158.4 5.2 %pad_maximum_fusion = f32[12,320,320]{2,1,0:T(8,128)} fusion(f32[3,320,320]{2,1,0:T(8,128)S(1)} %bitcast.54, f32[9,320,320]{2,1,0:T(8,128)} %bitcast.52), kind=kLoop, calls=%fused_computation.2 | loop fusion | flops 1228800 | bytes 9830400 | tf_op jit(solution)/shard_map/concatenate | solution.py:82
  163.6 0.0 all-reduce.4.cloned.1.call-update
  163.6 0.0 all-reduce.6.cloned.1.call-start
  163.7 250.9 %all-reduce.4.cloned.1.call-done = f32[12,320,320]{2,1,0:T(8,128)} async-done(((f32[12,320,320]{2,1,0:T(8,128)}), f32[12,320,320]{2,1,0:T(8,128)}) %all-reduce.4.cloned.1.call-update) | async-done | bytes 4915216 | tf_op jit(solution)/shard_map/psum | solution.py:85
  414.5 0.0 all-reduce.6.cloned.1.call-update
  414.6 41.3 %all-reduce.6.cloned.1.call-done = f32[12,320,320]{2,1,0:T(8,128)} async-done(((f32[12,320,320]{2,1,0:T(8,128)}), f32[12,320,320]{2,1,0:T(8,128)}) %all-reduce.6.cloned.1.call-update) | async-done | bytes 4915216 | tf_op jit(solution)/shard_map/psum | solution.py:85
  455.9 0.0 copy-start.1
  455.9 4.8 %slice_multiply_fusion = f32[9,320,320]{2,1,0:T(8,128)} fusion(f32[12,320,320]{2,1,0:T(8,128)} %all-reduce.6.cloned.1.call-done), kind=kLoop, calls=%fused_computation.5 | loop fusion | flops 921600 | bytes 7372800 | tf_op jit(solution)/shard_map/mul | solution.py:88
  460.6 2.6 slice_multiply_fusion.2
  463.3 0.0 copy-done.1
Async XLA Ops:
  7.2 111.7 %copy-start = (bf16[3,320,320]{2,1,0:T(8,128)(2,1)S(1)}, bf16[3,320,320]{2,1,0:T(8,128)(2,1)}, u32[]{:S(2)}) copy-start(bf16[3,320,320]{2,1,0:T(8,128)(2,1)} %param.9) | copy-start | bytes 1843204
  7.2 407.4 %all-reduce.4.cloned.1.call-start = ((), (), s32[]{:S(2)}) async-start(), calls=%async_computation | async-start | bytes 11796480 | tf_op jit(solution)/shard_map/psum | solution.py:85
  8.5 20.8 %collective-permute-start = (bf16[2,4,1,64,320]{4,3,2,1,0:T(8,128)(2,1)S(1)}, bf16[2,4,1,64,320]{4,3,2,1,0:T(8,128)(2,1)S(1)}, u32[]{:S(2)}, u32[]{:S(2)}) collective-permute-start(bf16[2,4,1,64,320]{4,3,2,1,0:T(8,128)(2,1)S(1)} %get-tuple-element.24), channel_id=1, source_target_pairs={{0,1},{1,2},{2,3},{3,4},{4,5},{5,6},{6,7},{7,8},{8,9},{9,10},{10,1... | collective-permute-start | bytes 983048 | tf_op jit(solution)/shard_map/ppermute | solution.py:15
  12.6 16.8 %collective-permute-start.1 = (bf16[2,4,1,64,320]{4,3,2,1,0:T(8,128)(2,1)S(1)}, bf16[2,4,1,64,320]{4,3,2,1,0:T(8,128)(2,1)S(1)}, u32[]{:S(2)}, u32[]{:S(2)}) collective-permute-start(bf16[2,4,1,64,320]{4,3,2,1,0:T(8,128)(2,1)S(1)} %get-tuple-element.25), channel_id=1, source_target_pairs={{1,0},{2,1},{3,2},{4,3},{5,4},{6,5},{7,6},{8,7},{9,8},{10,9},{11,1... | collective-permute-start | bytes 983048 | tf_op jit(solution)/shard_map/ppermute | solution.py:17
  31.7 4.9 %copy-start.2 = (bf16[2,4,4,64,320]{4,3,2,1,0:T(8,128)(2,1)S(1)}, bf16[2,4,4,64,320]{4,3,2,1,0:T(8,128)(2,1)}, u32[]{:S(2)}) copy-start(bf16[2,4,4,64,320]{4,3,2,1,0:T(8,128)(2,1)} %param.5) | copy-start | bytes 3932164
  72.3 2.3 copy-start.3
  74.6 6.8 %copy-start.4 = (bf16[3,320,320]{2,1,0:T(8,128)(2,1)S(1)}, bf16[3,320,320]{2,1,0:T(8,128)(2,1)}, u32[]{:S(2)}) copy-start(bf16[3,320,320]{2,1,0:T(8,128)(2,1)} %param.7) | copy-start | bytes 1843204
  74.9 22.3 %collective-permute-start.2 = (bf16[2,2,1,4,64,320]{5,4,3,2,1,0:T(8,128)(2,1)S(1)}, bf16[2,2,1,4,64,320]{5,4,3,2,1,0:T(8,128)(2,1)S(1)}, u32[]{:S(2)}, u32[]{:S(2)}) collective-permute-start(bf16[2,2,1,4,64,320]{5,4,3,2,1,0:T(8,128)(2,1)S(1)} %get-tuple-element.6), channel_id=1, source_target_pairs={{0,16},{16,32},{32,48},{48,64},{64,80},{80,96},{96,112},{1,17},{17... | collective-permute-start | bytes 1966088 | tf_op jit(solution)/shard_map/ppermute | solution.py:15
  79.2 33.8 %collective-permute-start.3 = (bf16[2,2,1,4,64,320]{5,4,3,2,1,0:T(8,128)(2,1)S(1)}, bf16[2,2,1,4,64,320]{5,4,3,2,1,0:T(8,128)(2,1)S(1)}, u32[]{:S(2)}, u32[]{:S(2)}) collective-permute-start(bf16[2,2,1,4,64,320]{5,4,3,2,1,0:T(8,128)(2,1)S(1)} %get-tuple-element.7), channel_id=1, source_target_pairs={{16,0},{32,16},{48,32},{64,48},{80,64},{96,80},{112,96},{17,1},{33... | collective-permute-start | bytes 1966088 | tf_op jit(solution)/shard_map/ppermute | solution.py:17
  121.5 9.7 %copy-start.5 = (bf16[2,4,4,64,320]{4,3,2,1,0:T(8,128)(2,1)}, bf16[2,4,4,64,320]{4,3,2,1,0:T(8,128)(2,1)S(1)}, u32[]{:S(2)}) copy-start(bf16[2,4,4,64,320]{4,3,2,1,0:T(8,128)(2,1)S(1)} %add_convert_fusion) | copy-start | bytes 3932164
  121.6 14.8 %collective-permute-start.4 = (bf16[2,1,4,64,320]{4,3,2,1,0:T(8,128)(2,1)S(1)}, bf16[2,1,4,64,320]{4,3,2,1,0:T(8,128)(2,1)S(1)}, u32[]{:S(2)}, u32[]{:S(2)}) collective-permute-start(bf16[2,1,4,64,320]{4,3,2,1,0:T(8,128)(2,1)S(1)} %get-tuple-element.20), channel_id=1, source_target_pairs={{16,0},{32,16},{48,32},{64,48},{80,64},{96,80},{112,96},{17,1},{33... | collective-permute-start | bytes 983048 | tf_op jit(solution)/shard_map/ppermute | solution.py:17
  125.0 15.1 %collective-permute-start.5 = (bf16[2,1,4,64,320]{4,3,2,1,0:T(8,128)(2,1)S(1)}, bf16[2,1,4,64,320]{4,3,2,1,0:T(8,128)(2,1)S(1)}, u32[]{:S(2)}, u32[]{:S(2)}) collective-permute-start(bf16[2,1,4,64,320]{4,3,2,1,0:T(8,128)(2,1)S(1)} %get-tuple-element.21), channel_id=1, source_target_pairs={{0,16},{16,32},{32,48},{48,64},{64,80},{80,96},{96,112},{1,17},{17... | collective-permute-start | bytes 983048 | tf_op jit(solution)/shard_map/ppermute | solution.py:15
  140.1 0.7 copy-start.6
  163.6 292.2 %all-reduce.6.cloned.1.call-start = ((), (), s32[]{:S(2)}) async-start(), calls=%async_computation.1 | async-start | bytes 11796480 | tf_op jit(solution)/shard_map/psum | solution.py:85
  455.9 7.4 %copy-start.1 = (bf16[3,320,320]{2,1,0:T(8,128)(2,1)S(1)}, bf16[3,320,320]{2,1,0:T(8,128)(2,1)}, u32[]{:S(2)}) copy-start(bf16[3,320,320]{2,1,0:T(8,128)(2,1)} %param.9) | copy-start | bytes 1843204
Sparse Core Ops, SparseCore 0:
  163.8 250.7 all-reduce.3
  417.3 38.4 all-reduce.5
